TPU v7x, 32 devices: a whole 2x2x4 slice. The times are simulated.
32 devices in a mesh: section: 4 (over y, core), ep: 8 (over z, x).
Axes of the slice: x: 2, y: 2, z: 4, core: 2. Of those that a mesh axis runs over, the one named last changes fastest.
Arguments:
- rows_in: bfloat16 [4, 64, 7168], P(None, 'ep'), may hold values from -6 to 6
- routes: int32 [4, 4, 64, 2], P('section', None, 'ep'), may hold values from 0 to 3, all different within a row; in each aligned block of 8 rows (0 to 7, 8 to 15, ..., all dimensions but the last counted through in order) at most 4 rows name the same one
- hot_blocks: int32 [4], P('section'), may hold values from 0 to 15
- gains: float32 [4, 7168], P('section'), may hold values from 0.1 to 1.9
- router: bfloat16 [4, 7168, 4], P('section'), may hold values from -0.0625 to 0.0625
- w_gate: bfloat16 [4, 7168, 4096], P('section', None, 'ep'), may hold values from -0.0625 to 0.0625
- w_up: bfloat16 [4, 7168, 4096], P('section', None, 'ep'), may hold values from -0.0625 to 0.0625
- w_down: bfloat16 [4, 4096, 7168], P('section', 'ep'), may hold values from -0.1875 to 0.1875
Outputs:
- section_rows: bfloat16 [4, 4, 64, 7168], P('section', None, 'ep')
- relative_load: float32 [4, 8], P('section', 'ep')
Inputs may be any that keep to these rules, and one draw needn't show every extreme that they name: `routes`: in every layer and micro-batch the 8 rows of one device name each expert at most 4 times.
All inputs are finite; a program needn't handle non-finite values.
Results may differ from a plain program's by a relative error of at most 0.025.
Values may be sent and summed in bfloat16 or wider, within the bound.
A program may use at most 128 MiB of HBM per device.

v0:
```python
import jax
import jax.numpy as jnp
from jax import lax
from jax.sharding import PartitionSpec as P

FFW = 1024
BLK = 256


def spread(block, axis, source):
    block = jnp.where(lax.axis_index(axis) == source, block, jnp.zeros_like(block))
    return lax.psum(block, axis)


def shifted(block, axis, distance):
    devices = range(lax.axis_size(axis))
    route = [(i - distance, i) for i in devices if i - distance in devices]
    return lax.ppermute(block, axis, route)


def local(rows_in, routes, hot_blocks, gains, router, w_gate, w_up, w_down):
    section_index = lax.axis_index("section")
    ep_index = lax.axis_index("ep")
    section_count = lax.axis_size("section")
    micro_count = rows_in.shape[0]
    tok_rows = rows_in.shape[1]
    model_width = rows_in.shape[2]
    columns = w_gate.shape[2]
    expert_count = router.shape[2]
    top_count = routes.shape[3]
    capacity = tok_rows // 2
    blocks_per_expert = FFW // BLK
    hot_index = hot_blocks[0]
    owner_index = hot_index // 2
    hot_expert = hot_index // blocks_per_expert
    norm_gain = gains[0]
    router_w = router[0]
    gate_w = w_gate[0]
    up_w = w_up[0]
    down_w = w_down[0]
    column_block = 2 * ep_index + lax.iota(jnp.int32, columns) // BLK
    keep_column = (column_block != hot_index)[None, :]
    expert_ids = lax.iota(jnp.int32, expert_count)
    block_start = hot_index % 2 * BLK
    copy_gate, copy_up, copy_down = (
        spread(lax.dynamic_slice_in_dim(gate_w, block_start, BLK, 1), "ep", owner_index),
        spread(lax.dynamic_slice_in_dim(up_w, block_start, BLK, 1), "ep", owner_index),
        spread(lax.dynamic_slice_in_dim(down_w, block_start, BLK, 0), "ep", owner_index),
    )

    def expert_rows(flat_rows):
        gate_value = jnp.dot(flat_rows, gate_w, preferred_element_type=jnp.float32)
        up_value = jnp.dot(flat_rows, up_w, preferred_element_type=jnp.float32)
        activation = (jax.nn.silu(gate_value) * up_value).astype(jnp.bfloat16)
        home_act = jnp.where(keep_column, activation, jnp.zeros_like(activation))
        return jnp.dot(home_act, down_w, preferred_element_type=jnp.float32).astype(jnp.bfloat16)

    def work_both(recv_parts):
        recv_rows, recv_flags = recv_parts
        sources = recv_rows.shape[0]
        item_count = recv_rows.shape[1]
        home_part = expert_rows(recv_rows.reshape(sources * item_count, model_width))
        home_part = home_part.reshape(sources, item_count, model_width)
        returned = lax.all_to_all(home_part, "ep", split_axis=0, concat_axis=0, tiled=True)
        filled = jnp.sum(recv_flags.astype(jnp.float32), axis=0, keepdims=True)
        return (returned, filled)

    def apply_layer(layer_input, route_ids):
        rows_float = layer_input.astype(jnp.float32)
        mean_square = jnp.mean(rows_float * rows_float, axis=-1, keepdims=True)
        normed = (rows_float * lax.rsqrt(mean_square + 1e-06) * norm_gain).astype(jnp.bfloat16)
        scores = jax.nn.sigmoid(jnp.dot(normed, router_w, preferred_element_type=jnp.float32))
        member = (route_ids[:, :, None] == expert_ids[None, None, :]).astype(jnp.float32)
        chosen = jnp.sum(member * scores[:, None, :], axis=2)
        gate_weights = 2.5 * chosen / jnp.sum(chosen, axis=1, keepdims=True)
        token_gate = jnp.sum(member * gate_weights[:, :, None], axis=1)
        routed = jnp.sum(member, axis=1)
        slot_rank = jnp.cumsum(routed, axis=0) - routed
        slot_ids = lax.iota(jnp.float32, capacity)
        placement = routed.T[:, None, :] * (
            slot_rank.T[:, None, :] == slot_ids[None, :, None]
        ).astype(jnp.float32)
        packed = jnp.einsum(
            "ect,tf->ecf",
            placement.astype(jnp.bfloat16),
            normed,
            preferred_element_type=jnp.float32,
        ).astype(jnp.bfloat16)
        slot_flags = jnp.sum(placement, axis=2).astype(jnp.bfloat16)
        send_rows = jnp.repeat(packed, 2, axis=0)
        send_flags = jnp.repeat(slot_flags, 2, axis=0)
        home_back, filled = work_both(
            (
                lax.all_to_all(send_rows, "ep", split_axis=0, concat_axis=0, tiled=True),
                lax.all_to_all(send_flags, "ep", split_axis=0, concat_axis=0, tiled=True),
            )
        )
        combined = home_back.astype(jnp.float32).reshape(expert_count, 2, capacity, model_width)
        pair_sum = combined[:, 0] + combined[:, 1]
        weighting = placement * token_gate.T[:, None, :]
        routed_sum = jnp.einsum("ect,ecf->tf", weighting, pair_sum, precision=lax.Precision.HIGHEST)
        local_gate = jnp.dot(normed, copy_gate, preferred_element_type=jnp.float32)
        local_up = jnp.dot(normed, copy_up, preferred_element_type=jnp.float32)
        local_act = (jax.nn.silu(local_gate) * local_up).astype(jnp.bfloat16)
        local_part = (
            jnp.dot(local_act, copy_down, preferred_element_type=jnp.float32)
            .astype(jnp.bfloat16)
            .astype(jnp.float32)
        )
        hot_gate = jnp.sum(jnp.where((expert_ids == hot_expert)[None, :], token_gate, 0.0), axis=1)
        routed_sum = routed_sum + hot_gate[:, None] * local_part
        own_hot = jnp.sum(jnp.where((expert_ids == hot_expert)[None, :], routed, 0.0))
        return ((rows_float + routed_sum).astype(jnp.bfloat16), jnp.sum(filled), own_hot)

    def run_tick(tick_index, loop_state):
        incoming, outputs, home_total, hot_total = loop_state
        micro_index = tick_index - section_index
        is_live = (micro_index >= 0) & (micro_index < micro_count)
        clipped = jnp.clip(micro_index, 0, micro_count - 1)
        fresh_rows = lax.dynamic_index_in_dim(rows_in, clipped, 0, keepdims=False)
        layer_input = jnp.where(section_index == 0, fresh_rows, incoming)
        route_ids = lax.dynamic_index_in_dim(routes[0], clipped, 0, keepdims=False)
        next_rows, home_rows, hot_rows = apply_layer(layer_input, route_ids)
        updated = lax.dynamic_update_index_in_dim(outputs, next_rows, clipped, 0)
        outputs = jnp.where(is_live, updated, outputs)
        home_total = home_total + jnp.where(is_live, home_rows, 0.0)
        hot_total = hot_total + jnp.where(is_live, hot_rows, 0.0)
        incoming = shifted(next_rows, "section", 1)
        return (incoming, outputs, home_total, hot_total)

    tick_count = micro_count + section_count - 1
    start_state = (
        jnp.zeros((tok_rows, model_width), jnp.bfloat16),
        jnp.zeros(rows_in.shape, jnp.bfloat16),
        jnp.float32(0.0),
        jnp.float32(0.0),
    )
    final_state = lax.fori_loop(0, tick_count, run_tick, start_state)
    outputs = final_state[1]
    unit_count = (
        final_state[2] * (2.0 - (owner_index == ep_index).astype(jnp.float32)) + final_state[3]
    )
    relative = unit_count / float(micro_count * tok_rows * top_count * blocks_per_expert)
    return (outputs[None], relative.reshape(1, 1))


def solution(mesh):
    return jax.shard_map(
        local,
        mesh=mesh,
        in_specs=(
            P(None, "ep", None),
            P("section", None, "ep", None),
            P("section"),
            P("section", None),
            P("section", None, None),
            P("section", None, "ep"),
            P("section", None, "ep"),
            P("section", "ep", None),
        ),
        out_specs=(P("section", None, "ep", None), P("section", "ep")),
        check_vma=False,
    )
```

profile of v0, /device:TPU:0, one launch (start us, length us, event | category | flops | bytes accessed | tf_op | source)
XLA Modules:
  0.0 818.4 jit_solution(853677512756800073)
XLA Ops:
  12.7 6.4 select_bitcast_fusion.1
  19.2 343.5 %all-reduce.3.cloned.1.call-done = (bf16[7168,256]{1,0:T(8,128)(2,1)}, bf16[7168,256]{1,0:T(8,128)(2,1)}, bf16[256,7168]{1,0:T(8,128)(2,1)}) async-done(((bf16[7168,256]{1,0:T(8,128)(2,1)}, bf16[7168,256]{1,0:T(8,128)(2,1)}, bf16[256,7168]{1,0:T(8,128)(2,1)}), (bf16[7168,256]{1,0:T(8,128)(2,1)}, bf16[7168,256]{1,0:T(8,128)(2,1)}, bf16[256,7168]{1,0:T(8,128)(2,1)})) %all-reduce.3.cloned.1.call-update) | async-done | bytes 11010064 | tf_op jit(solution)/shard_map/psum | solution.py:12
  362.8 446.8 %while.22 = (s32[]{:T(128)}, bf16[8,7168]{1,0:T(8,128)(2,1)S(1)}, bf16[4,8,7168]{2,1,0:T(8,128)(2,1)S(1)}, f32[]{:T(128)}, f32[]{:T(128)}, /*index=5*/pred[]{:T(...) while((s32[]{:T(128)}, bf16[8,7168]{1,0:T(8,128)(2,1)S(1)}, ...), condition=%wide.region_14.15_spmd.clone.clone, body=%wide.region_3.14_spmd.clone.clone.sunk | while | flops 808455232 | bytes 45640856 | solution.py:138
  371.2 11.8 %all-to-all-done = bf16[8,4,7168]{2,1,0:T(4,128)(2,1)S(1)} async-done(((bf16[8,4,7168]{2,1,0:T(4,128)(2,1)}), bf16[8,4,7168]{2,1,0:T(4,128)(2,1)S(1)}, u32[]{:S(2)}, u32[]{:S(2)}) %all-to-all-start) | async-done | bytes 458784 | tf_op jit(solution)/shard_map/while/body/eval_jaxpr/all_to_all | solution.py:94
  387.5 7.9 convolution_convert_fusion.6
  421.4 5.9 all-to-all-done.2
  436.8 12.2 %all-to-all-done = bf16[8,4,7168]{2,1,0:T(4,128)(2,1)S(1)} async-done(((bf16[8,4,7168]{2,1,0:T(4,128)(2,1)}), bf16[8,4,7168]{2,1,0:T(4,128)(2,1)S(1)}, u32[]{:S(2)}, u32[]{:S(2)}) %all-to-all-start) | async-done | bytes 458784 | tf_op jit(solution)/shard_map/while/body/eval_jaxpr/all_to_all | solution.py:94
  453.6 7.9 convolution_convert_fusion.6
  487.5 5.9 all-to-all-done.2
  502.9 10.7 %all-to-all-done = bf16[8,4,7168]{2,1,0:T(4,128)(2,1)S(1)} async-done(((bf16[8,4,7168]{2,1,0:T(4,128)(2,1)}), bf16[8,4,7168]{2,1,0:T(4,128)(2,1)S(1)}, u32[]{:S(2)}, u32[]{:S(2)}) %all-to-all-start) | async-done | bytes 458784 | tf_op jit(solution)/shard_map/while/body/eval_jaxpr/all_to_all | solution.py:94
  518.1 7.9 convolution_convert_fusion.6
  550.7 5.9 all-to-all-done.2
  566.1 10.5 %all-to-all-done = bf16[8,4,7168]{2,1,0:T(4,128)(2,1)S(1)} async-done(((bf16[8,4,7168]{2,1,0:T(4,128)(2,1)}), bf16[8,4,7168]{2,1,0:T(4,128)(2,1)S(1)}, u32[]{:S(2)}, u32[]{:S(2)}) %all-to-all-start) | async-done | bytes 458784 | tf_op jit(solution)/shard_map/while/body/eval_jaxpr/all_to_all | solution.py:94
  581.1 7.9 convolution_convert_fusion.6
  613.6 5.9 all-to-all-done.2
  629.1 10.5 %all-to-all-done = bf16[8,4,7168]{2,1,0:T(4,128)(2,1)S(1)} async-done(((bf16[8,4,7168]{2,1,0:T(4,128)(2,1)}), bf16[8,4,7168]{2,1,0:T(4,128)(2,1)S(1)}, u32[]{:S(2)}, u32[]{:S(2)}) %all-to-all-start) | async-done | bytes 458784 | tf_op jit(solution)/shard_map/while/body/eval_jaxpr/all_to_all | solution.py:94
  644.0 7.9 convolution_convert_fusion.6
  676.6 5.9 all-to-all-done.2
  692.0 10.5 %all-to-all-done = bf16[8,4,7168]{2,1,0:T(4,128)(2,1)S(1)} async-done(((bf16[8,4,7168]{2,1,0:T(4,128)(2,1)}), bf16[8,4,7168]{2,1,0:T(4,128)(2,1)S(1)}, u32[]{:S(2)}, u32[]{:S(2)}) %all-to-all-start) | async-done | bytes 458784 | tf_op jit(solution)/shard_map/while/body/eval_jaxpr/all_to_all | solution.py:94
  707.0 7.9 convolution_convert_fusion.6
  739.6 5.9 all-to-all-done.2
  755.0 10.5 %all-to-all-done = bf16[8,4,7168]{2,1,0:T(4,128)(2,1)S(1)} async-done(((bf16[8,4,7168]{2,1,0:T(4,128)(2,1)}), bf16[8,4,7168]{2,1,0:T(4,128)(2,1)S(1)}, u32[]{:S(2)}, u32[]{:S(2)}) %all-to-all-start) | async-done | bytes 458784 | tf_op jit(solution)/shard_map/while/body/eval_jaxpr/all_to_all | solution.py:94
  770.0 7.9 convolution_convert_fusion.6
  802.5 5.9 all-to-all-done.2
  (251 shorter events, 270.4 us)
Async XLA Ops:
  7.2 355.6 %all-reduce.3.cloned.1.call-start = ((), (), s32[]{:S(2)}) async-start(), calls=%async_computation.3 | async-start | bytes 22020096 | tf_op jit(solution)/shard_map/psum | solution.py:12
  366.3 16.7 %all-to-all-start = ((bf16[8,4,7168]{2,1,0:T(4,128)(2,1)}), bf16[8,4,7168]{2,1,0:T(4,128)(2,1)S(1)}, u32[]{:S(2)}, u32[]{:S(2)}) async-start(bf16[8,4,7168]{2,1,0:T(4,128)(2,1)} %bitcast.92), calls=%async_computation | async-start | bytes 917504 | tf_op jit(solution)/shard_map/while/body/eval_jaxpr/all_to_all | solution.py:94
  396.4 16.9 %all-to-all-start.1 = ((bf16[8,4,7168]{2,1,0:T(4,128)(2,1)}), bf16[8,4,7168]{2,1,0:T(4,128)(2,1)S(1)}, u32[]{:S(2)}, u32[]{:S(2)}) async-start(bf16[8,4,7168]{2,1,0:T(4,128)(2,1)} %reshape.177), calls=%async_computation.1 | async-start | bytes 917504 | tf_op jit(solution)/shard_map/while/body/eval_jaxpr/all_to_all | solution.py:64
  414.5 14.1 %collective-permute-start = (bf16[8,7168]{1,0:T(8,128)(2,1)S(1)}, bf16[8,7168]{1,0:T(8,128)(2,1)S(1)}, u32[]{:S(2)}, u32[]{:S(2)}) collective-permute-start(bf16[8,7168]{1,0:T(8,128)(2,1)S(1)} %get-tuple-element.674), channel_id=1, source_target_pairs={{0,8},{8,16},{16,24},{1,9},{9,17},{17,25},{2,10},{10,18},{18,26},{... | collective-permute-start | bytes 344072 | tf_op jit(solution)/shard_map/while/body/eval_jaxpr/ppermute | solution.py:18
  416.6 10.7 %all-to-all-start.2 = ((bf16[8,1,4]{2,1,0:T(2,128)(2,1)}), bf16[8,1,4]{2,1,0:T(2,128)(2,1)S(1)}, u32[]{:S(2)}, u32[]{:S(2)}) async-start(bf16[8,1,4]{2,1,0:T(2,128)(2,1)} %copy.40), calls=%async_computation.2 | async-start | bytes 8192 | tf_op jit(solution)/shard_map/while/body/eval_jaxpr/all_to_all | solution.py:95
  432.0 17.1 %all-to-all-start = ((bf16[8,4,7168]{2,1,0:T(4,128)(2,1)}), bf16[8,4,7168]{2,1,0:T(4,128)(2,1)S(1)}, u32[]{:S(2)}, u32[]{:S(2)}) async-start(bf16[8,4,7168]{2,1,0:T(4,128)(2,1)} %bitcast.92), calls=%async_computation | async-start | bytes 917504 | tf_op jit(solution)/shard_map/while/body/eval_jaxpr/all_to_all | solution.py:94
  462.4 16.9 %all-to-all-start.1 = ((bf16[8,4,7168]{2,1,0:T(4,128)(2,1)}), bf16[8,4,7168]{2,1,0:T(4,128)(2,1)S(1)}, u32[]{:S(2)}, u32[]{:S(2)}) async-start(bf16[8,4,7168]{2,1,0:T(4,128)(2,1)} %reshape.177), calls=%async_computation.1 | async-start | bytes 917504 | tf_op jit(solution)/shard_map/while/body/eval_jaxpr/all_to_all | solution.py:64
  480.6 14.1 %collective-permute-start = (bf16[8,7168]{1,0:T(8,128)(2,1)S(1)}, bf16[8,7168]{1,0:T(8,128)(2,1)S(1)}, u32[]{:S(2)}, u32[]{:S(2)}) collective-permute-start(bf16[8,7168]{1,0:T(8,128)(2,1)S(1)} %get-tuple-element.674), channel_id=1, source_target_pairs={{0,8},{8,16},{16,24},{1,9},{9,17},{17,25},{2,10},{10,18},{18,26},{... | collective-permute-start | bytes 344072 | tf_op jit(solution)/shard_map/while/body/eval_jaxpr/ppermute | solution.py:18
  482.7 10.7 %all-to-all-start.2 = ((bf16[8,1,4]{2,1,0:T(2,128)(2,1)}), bf16[8,1,4]{2,1,0:T(2,128)(2,1)S(1)}, u32[]{:S(2)}, u32[]{:S(2)}) async-start(bf16[8,1,4]{2,1,0:T(2,128)(2,1)} %copy.40), calls=%async_computation.2 | async-start | bytes 8192 | tf_op jit(solution)/shard_map/while/body/eval_jaxpr/all_to_all | solution.py:95
  498.1 15.5 %all-to-all-start = ((bf16[8,4,7168]{2,1,0:T(4,128)(2,1)}), bf16[8,4,7168]{2,1,0:T(4,128)(2,1)S(1)}, u32[]{:S(2)}, u32[]{:S(2)}) async-start(bf16[8,4,7168]{2,1,0:T(4,128)(2,1)} %bitcast.92), calls=%async_computation | async-start | bytes 917504 | tf_op jit(solution)/shard_map/while/body/eval_jaxpr/all_to_all | solution.py:94
  526.9 16.2 %all-to-all-start.1 = ((bf16[8,4,7168]{2,1,0:T(4,128)(2,1)}), bf16[8,4,7168]{2,1,0:T(4,128)(2,1)S(1)}, u32[]{:S(2)}, u32[]{:S(2)}) async-start(bf16[8,4,7168]{2,1,0:T(4,128)(2,1)} %reshape.177), calls=%async_computation.1 | async-start | bytes 917504 | tf_op jit(solution)/shard_map/while/body/eval_jaxpr/all_to_all | solution.py:64
  544.4 13.4 %collective-permute-start = (bf16[8,7168]{1,0:T(8,128)(2,1)S(1)}, bf16[8,7168]{1,0:T(8,128)(2,1)S(1)}, u32[]{:S(2)}, u32[]{:S(2)}) collective-permute-start(bf16[8,7168]{1,0:T(8,128)(2,1)S(1)} %get-tuple-element.674), channel_id=1, source_target_pairs={{0,8},{8,16},{16,24},{1,9},{9,17},{17,25},{2,10},{10,18},{18,26},{... | collective-permute-start | bytes 344072 | tf_op jit(solution)/shard_map/while/body/eval_jaxpr/ppermute | solution.py:18
  561.2 15.3 %all-to-all-start = ((bf16[8,4,7168]{2,1,0:T(4,128)(2,1)}), bf16[8,4,7168]{2,1,0:T(4,128)(2,1)S(1)}, u32[]{:S(2)}, u32[]{:S(2)}) async-start(bf16[8,4,7168]{2,1,0:T(4,128)(2,1)} %bitcast.92), calls=%async_computation | async-start | bytes 917504 | tf_op jit(solution)/shard_map/while/body/eval_jaxpr/all_to_all | solution.py:94
  589.9 16.2 %all-to-all-start.1 = ((bf16[8,4,7168]{2,1,0:T(4,128)(2,1)}), bf16[8,4,7168]{2,1,0:T(4,128)(2,1)S(1)}, u32[]{:S(2)}, u32[]{:S(2)}) async-start(bf16[8,4,7168]{2,1,0:T(4,128)(2,1)} %reshape.177), calls=%async_computation.1 | async-start | bytes 917504 | tf_op jit(solution)/shard_map/while/body/eval_jaxpr/all_to_all | solution.py:64
  607.3 13.4 %collective-permute-start = (bf16[8,7168]{1,0:T(8,128)(2,1)S(1)}, bf16[8,7168]{1,0:T(8,128)(2,1)S(1)}, u32[]{:S(2)}, u32[]{:S(2)}) collective-permute-start(bf16[8,7168]{1,0:T(8,128)(2,1)S(1)} %get-tuple-element.674), channel_id=1, source_target_pairs={{0,8},{8,16},{16,24},{1,9},{9,17},{17,25},{2,10},{10,18},{18,26},{... | collective-permute-start | bytes 344072 | tf_op jit(solution)/shard_map/while/body/eval_jaxpr/ppermute | solution.py:18
  624.2 15.3 %all-to-all-start = ((bf16[8,4,7168]{2,1,0:T(4,128)(2,1)}), bf16[8,4,7168]{2,1,0:T(4,128)(2,1)S(1)}, u32[]{:S(2)}, u32[]{:S(2)}) async-start(bf16[8,4,7168]{2,1,0:T(4,128)(2,1)} %bitcast.92), calls=%async_computation | async-start | bytes 917504 | tf_op jit(solution)/shard_map/while/body/eval_jaxpr/all_to_all | solution.py:94
  652.9 16.2 %all-to-all-start.1 = ((bf16[8,4,7168]{2,1,0:T(4,128)(2,1)}), bf16[8,4,7168]{2,1,0:T(4,128)(2,1)S(1)}, u32[]{:S(2)}, u32[]{:S(2)}) async-start(bf16[8,4,7168]{2,1,0:T(4,128)(2,1)} %reshape.177), calls=%async_computation.1 | async-start | bytes 917504 | tf_op jit(solution)/shard_map/while/body/eval_jaxpr/all_to_all | solution.py:64
  670.3 13.4 %collective-permute-start = (bf16[8,7168]{1,0:T(8,128)(2,1)S(1)}, bf16[8,7168]{1,0:T(8,128)(2,1)S(1)}, u32[]{:S(2)}, u32[]{:S(2)}) collective-permute-start(bf16[8,7168]{1,0:T(8,128)(2,1)S(1)} %get-tuple-element.674), channel_id=1, source_target_pairs={{0,8},{8,16},{16,24},{1,9},{9,17},{17,25},{2,10},{10,18},{18,26},{... | collective-permute-start | bytes 344072 | tf_op jit(solution)/shard_map/while/body/eval_jaxpr/ppermute | solution.py:18
  687.2 15.3 %all-to-all-start = ((bf16[8,4,7168]{2,1,0:T(4,128)(2,1)}), bf16[8,4,7168]{2,1,0:T(4,128)(2,1)S(1)}, u32[]{:S(2)}, u32[]{:S(2)}) async-start(bf16[8,4,7168]{2,1,0:T(4,128)(2,1)} %bitcast.92), calls=%async_computation | async-start | bytes 917504 | tf_op jit(solution)/shard_map/while/body/eval_jaxpr/all_to_all | solution.py:94
  715.8 16.2 %all-to-all-start.1 = ((bf16[8,4,7168]{2,1,0:T(4,128)(2,1)}), bf16[8,4,7168]{2,1,0:T(4,128)(2,1)S(1)}, u32[]{:S(2)}, u32[]{:S(2)}) async-start(bf16[8,4,7168]{2,1,0:T(4,128)(2,1)} %reshape.177), calls=%async_computation.1 | async-start | bytes 917504 | tf_op jit(solution)/shard_map/while/body/eval_jaxpr/all_to_all | solution.py:64
  733.3 13.4 %collective-permute-start = (bf16[8,7168]{1,0:T(8,128)(2,1)S(1)}, bf16[8,7168]{1,0:T(8,128)(2,1)S(1)}, u32[]{:S(2)}, u32[]{:S(2)}) collective-permute-start(bf16[8,7168]{1,0:T(8,128)(2,1)S(1)} %get-tuple-element.674), channel_id=1, source_target_pairs={{0,8},{8,16},{16,24},{1,9},{9,17},{17,25},{2,10},{10,18},{18,26},{... | collective-permute-start | bytes 344072 | tf_op jit(solution)/shard_map/while/body/eval_jaxpr/ppermute | solution.py:18
  750.1 15.3 %all-to-all-start = ((bf16[8,4,7168]{2,1,0:T(4,128)(2,1)}), bf16[8,4,7168]{2,1,0:T(4,128)(2,1)S(1)}, u32[]{:S(2)}, u32[]{:S(2)}) async-start(bf16[8,4,7168]{2,1,0:T(4,128)(2,1)} %bitcast.92), calls=%async_computation | async-start | bytes 917504 | tf_op jit(solution)/shard_map/while/body/eval_jaxpr/all_to_all | solution.py:94
  778.8 16.2 %all-to-all-start.1 = ((bf16[8,4,7168]{2,1,0:T(4,128)(2,1)}), bf16[8,4,7168]{2,1,0:T(4,128)(2,1)S(1)}, u32[]{:S(2)}, u32[]{:S(2)}) async-start(bf16[8,4,7168]{2,1,0:T(4,128)(2,1)} %reshape.177), calls=%async_computation.1 | async-start | bytes 917504 | tf_op jit(solution)/shard_map/while/body/eval_jaxpr/all_to_all | solution.py:64
  796.2 13.4 %collective-permute-start = (bf16[8,7168]{1,0:T(8,128)(2,1)S(1)}, bf16[8,7168]{1,0:T(8,128)(2,1)S(1)}, u32[]{:S(2)}, u32[]{:S(2)}) collective-permute-start(bf16[8,7168]{1,0:T(8,128)(2,1)S(1)} %get-tuple-element.674), channel_id=1, source_target_pairs={{0,8},{8,16},{16,24},{1,9},{9,17},{17,25},{2,10},{10,18},{18,26},{... | collective-permute-start | bytes 344072 | tf_op jit(solution)/shard_map/while/body/eval_jaxpr/ppermute | solution.py:18
  (9 other events, 743.2 us)
Sparse Core Ops, SparseCore 0:
  19.3 343.4 all-reduce.2
where the time goes:
time: 821 us; the launch traced here: 818 us
  waiting for transfers between devices  495 us (60%)
  matrix products  152 us (19%)
  starting transfers between devices  85.9 us (10%)
  other arithmetic  35.9 us (4%)
  local copies, waits for them, and re-layouts  24.2 us (3%)
  between operations  15.9 us (2%)
  loops' own time  9.38 us (1%)
    psum x1, waiting for transfers between devices, spread(): return lax.psum(block, axis)  344 us
    all_to_all x7, waiting for transfers between devices, apply_layer(): lax.all_to_all(send_rows, 'ep', split_axis=0, concat_axis=0, tiled=True)  76.5 us
    dot_general x7, matrix products, expert_rows(): jnp.dot(home_act, down_w, preferred_element_type=jnp.float32)  55.2 us
    all_to_all x7, waiting for transfers between devices, apply_layer(): lax.all_to_all(send_flags, 'ep', split_axis=0, concat_axis=0, tiled=True)  41 us
    dot_general x7, matrix products, apply_layer(): jnp.dot(local_act, copy_down, preferred_element_type=jnp.float32)  36.9 us
    all_to_all x7, waiting for transfers between devices, work_both(): lax.all_to_all(home_part, 'ep', split_axis=0, concat_axis=0, tiled=True)  33.6 us
    dot_general x7, matrix products, expert_rows(): gate_value = jnp.dot(flat_rows, gate_w, preferred_element_type=jnp.float32)  31 us
    all_to_all x7, starting transfers between devices, apply_layer(): lax.all_to_all(send_flags, 'ep', split_axis=0, concat_axis=0, tiled=True)  26.7 us
  transfers between devices with their start and end apart: 29, of which 22 were waited for; matrix products, arithmetic and copies ran while one was open for 9% of the time, Pallas kernels for 0%

commit v1 on v0

--- a/solution.py
+++ b/solution.py
@@ -7,9 +7,14 @@
 BLK = 256
 
 
+def slot_drive(u, mesh_ax):
+    out_arr = lax.all_gather(u, axis_name=mesh_ax).sum(axis=0)
+    return out_arr
+
+
 def spread(block, axis, source):
     block = jnp.where(lax.axis_index(axis) == source, block, jnp.zeros_like(block))
-    return lax.psum(block, axis)
+    return slot_drive(block, axis)
 
 
 def shifted(block, axis, distance):

time: 821 us -> 2170 us (2.64)
  waiting for transfers between devices: 495 us -> 1800 us
  other arithmetic: 35.9 us -> 78.7 us
    all_gather x0 -> x3, waiting for transfers between devices: none -> 1650 us  [slot_drive(): out_arr = lax.all_gather(u, axis_name=mesh_ax).sum(axis=0)]
    psum x1 -> x0, waiting for transfers between devices: 344 us -> none  [spread(): return lax.psum(block, axis)]
    reduce_sum x0 -> x3, other arithmetic: none -> 39.5 us  [slot_drive(): out_arr = lax.all_gather(u, axis_name=mesh_ax).sum(axis=0)]
  transfers between devices with their start and end apart: 29 -> 31, of which waited for: 22 -> 24; matrix products, arithmetic and copies ran while one was open for 9% -> 5% of each run, Pallas kernels for 0% -> 0%
where the time goes in v1:
time: 2170 us; the launch traced here: 2160 us
  waiting for transfers between devices  1800 us (83%)
  matrix products  153 us (7%)
  starting transfers between devices  86.9 us (4%)
  other arithmetic  78.7 us (4%)
  local copies, waits for them, and re-layouts  24.2 us (1%)
    all_gather x3, waiting for transfers between devices, slot_drive(): out_arr = lax.all_gather(u, axis_name=mesh_ax).sum(axis=0)  1650 us
    all_to_all x7, waiting for transfers between devices, apply_layer(): lax.all_to_all(send_rows, 'ep', split_axis=0, concat_axis=0, tiled=True)  75.8 us
    dot_general x7, matrix products, expert_rows(): jnp.dot(home_act, down_w, preferred_element_type=jnp.float32)  55.2 us
  transfers between devices with their start and end apart: 31, of which 24 were waited for; matrix products, arithmetic and copies ran while one was open for 5% of the time, Pallas kernels for 0%

profile of v1, /device:TPU:0, one launch (start us, length us, event | category | flops | bytes accessed | tf_op | source)
XLA Modules:
  0.0 2164.9 jit_solution(12279119802482122645)
XLA Ops:
  21.8 552.5 %all-gather.4.cloned.1.call-done = bf16[8,7168,256]{2,1,0:T(8,128)(2,1)} async-done(((bf16[1,7168,256]{2,1,0:T(8,128)(2,1)}), bf16[8,7168,256]{2,1,0:T(8,128)(2,1)}) %all-gather.4.cloned.1.call-update) | async-done | bytes 29360144 | tf_op jit(solution)/shard_map/all_gather | solution.py:11
  574.3 13.3 reduce_sum.167
  587.6 547.2 %all-gather.6.cloned.1.call-done = bf16[8,7168,256]{2,1,0:T(8,128)(2,1)} async-done(((bf16[1,7168,256]{2,1,0:T(8,128)(2,1)}), bf16[8,7168,256]{2,1,0:T(8,128)(2,1)}) %all-gather.6.cloned.1.call-update) | async-done | bytes 29360144 | tf_op jit(solution)/shard_map/all_gather | solution.py:11
  1134.8 13.3 reduce_sum.168
  1148.2 547.2 %all-gather.8.cloned.1.call-done = bf16[8,256,7168]{2,1,0:T(8,128)(2,1)} async-done(((bf16[1,256,7168]{2,1,0:T(8,128)(2,1)}), bf16[8,256,7168]{2,1,0:T(8,128)(2,1)}) %all-gather.8.cloned.1.call-update) | async-done | bytes 29360144 | tf_op jit(solution)/shard_map/all_gather | solution.py:11
  1695.4 12.8 reduce_sum.169
  1708.3 448.1 %while.22 = (s32[]{:T(128)}, bf16[8,7168]{1,0:T(8,128)(2,1)S(1)}, bf16[4,8,7168]{2,1,0:T(8,128)(2,1)S(1)}, f32[]{:T(128)}, f32[]{:T(128)}, /*index=5*/pred[]{:T(...) while((s32[]{:T(128)}, bf16[8,7168]{1,0:T(8,128)(2,1)S(1)}, ...), condition=%wide.region_14.15_spmd.clone.clone, body=%wide.region_3.14_spmd.clone.clone.sunk | while | flops 808455232 | bytes 45640856 | solution.py:143
  1717.8 11.8 all-to-all-done
  1734.2 7.9 convolution_convert_fusion.6
  1768.2 5.7 all-to-all-done.2
  1783.6 12.1 all-to-all-done
  1800.3 7.9 convolution_convert_fusion.6
  1834.3 5.7 all-to-all-done.2
  1849.7 10.6 all-to-all-done
  1864.8 7.9 convolution_convert_fusion.6
  1912.9 10.3 all-to-all-done
  1927.8 7.9 convolution_convert_fusion.6
  1975.9 10.3 all-to-all-done
  1990.8 7.9 convolution_convert_fusion.6
  2023.5 5.7 all-to-all-done.2
  2038.9 10.3 all-to-all-done
  2053.8 7.9 convolution_convert_fusion.6
  2101.9 10.3 all-to-all-done
  2116.8 7.9 convolution_convert_fusion.6
  (259 shorter events, 304.3 us)
Async XLA Ops:
  7.2 567.1 %all-gather.4.cloned.1.call-start = ((), (), s32[]{:S(2)}) async-start(), calls=%async_computation.3 | async-start | bytes 33030144 | tf_op jit(solution)/shard_map/all_gather | solution.py:11
  12.4 1122.4 %all-gather.6.cloned.1.call-start = ((), (), s32[]{:S(2)}) async-start(), calls=%async_computation.4 | async-start | bytes 33030144 | tf_op jit(solution)/shard_map/all_gather | solution.py:11
  17.1 1678.3 %all-gather.8.cloned.1.call-start = ((), (), s32[]{:S(2)}) async-start(), calls=%async_computation.5 | async-start | bytes 33030144 | tf_op jit(solution)/shard_map/all_gather | solution.py:11
  1711.8 17.8 all-to-all-start
  1743.0 16.9 all-to-all-start.1
  1761.1 14.1 collective-permute-start
  1778.6 17.1 all-to-all-start
  1809.1 16.9 all-to-all-start.1
  1827.2 14.1 collective-permute-start
  1844.7 15.5 all-to-all-start
  1873.6 16.2 all-to-all-start.1
  1891.1 13.4 collective-permute-start
  1907.9 15.3 all-to-all-start
  1936.6 16.2 all-to-all-start.1
  1954.0 13.4 collective-permute-start
  1970.9 15.3 all-to-all-start
  1999.6 16.2 all-to-all-start.1
  2017.0 13.4 collective-permute-start
  2033.9 15.3 all-to-all-start
  2062.6 16.2 all-to-all-start.1
  2080.0 13.4 collective-permute-start
  2096.9 15.3 all-to-all-start
  2125.6 16.2 all-to-all-start.1
  2143.0 13.4 collective-permute-start
  (10 other events, 1192.7 us)
Sparse Core Ops, SparseCore 0:
  12.5 561.7 all-gather.3
  575.8 558.9 all-gather.5
  1136.4 558.9 all-gather.7
